TPU v7x, 256 devices: a whole 4x4x8 slice. The times are simulated.
256 devices in a mesh: segment: 4 (over x), shard: 64 (over y, z, core).
Axes of the slice: x: 4, y: 4, z: 8, core: 2. Of those that a mesh axis runs over, the one named last changes fastest.
Arguments:
- tokens: bfloat16 [3, 128, 3072], P(None, 'shard'), may hold values from -6 to 6
- norm_gain: float32 [4, 3072], P('segment'), may hold values from 0.5 to 1.5
- w_gate: bfloat16 [4, 3072, 32768], P('segment', None, 'shard'), may hold values from -0.109375 to 0.109375
- w_up: bfloat16 [4, 3072, 32768], P('segment', None, 'shard'), may hold values from -0.109375 to 0.109375
- w_down: bfloat16 [4, 32768, 3072], P('segment', 'shard'), may hold values from -0.046875 to 0.046875
- block_counts: int32 [4], P('segment'), may hold values from 1 to 2
- gate_prob: float32 [4, 3, 128], P('segment', None, 'shard'), may hold values from 0.1 to 1
Outputs:
- section_outputs: bfloat16 [4, 3, 128, 3072], P('segment', None, 'shard')
All inputs are finite; a program needn't handle non-finite values.
Results may differ from a plain program's by a relative error of at most 0.009.
Values may be sent and summed in bfloat16 or wider, within the bound.
A program may use at most 64 MiB of HBM per device.

v0:
```python
import jax
import jax.numpy as jnp
from jax import lax
from jax.sharding import PartitionSpec as P

FF = 16384


def shifted(value, axis, steps):
    count = lax.axis_size(axis)
    initial, last = (max(0, -steps), min(count, count - steps))
    return lax.ppermute(value, axis, [(source, source + steps) for source in range(initial, last)])


def normalize(rows, row_gain):
    values = rows.astype(jnp.float32)
    scale = lax.rsqrt(jnp.mean(values * values, axis=-1, keepdims=True) + 1e-05)
    return (values * scale * row_gain).astype(jnp.bfloat16)


def expert_rows(normed, gate_part, up_part, down_part):
    gate_val = jnp.dot(normed, gate_part, preferred_element_type=jnp.float32)
    up_val = jnp.dot(normed, up_part, preferred_element_type=jnp.float32)
    hidden = (jax.nn.silu(gate_val) * up_val).astype(jnp.bfloat16)
    return jnp.dot(hidden, down_part, preferred_element_type=jnp.float32)


def shards(tokens, norm_gain, w_gate, w_up, w_down, block_counts, gate_prob):
    segment_index = lax.axis_index("segment")
    segment_count = lax.axis_size("segment")
    shard_count = lax.axis_size("shard")
    hidden_count = w_gate.shape[2]
    own_expert = lax.axis_index("shard") // (FF // hidden_count)
    zero_blocks = block_counts[0]
    row_gain = norm_gain[0]
    gate_part = w_gate[0]
    up_part = w_up[0]
    down_part = w_down[0]
    probs = gate_prob[0]
    block_total = tokens.shape[0]
    local_rows = tokens.shape[1]
    width = tokens.shape[2]
    first_block = jnp.where(own_expert == 0, 0, zero_blocks)
    last_block = jnp.where(own_expert == 0, zero_blocks, block_total)
    carried = tokens
    stored = jnp.zeros_like(tokens)
    for tick in range(segment_count):
        normed = normalize(carried, row_gain)
        gathered = lax.all_gather(normed, "shard", axis=1, tiled=True)
        partial_sum = jnp.zeros(gathered.shape, jnp.float32)

        def add_block(block_id, acc):
            block_rows = lax.dynamic_index_in_dim(gathered, block_id, 0, keepdims=False)
            result = expert_rows(block_rows, gate_part, up_part, down_part)
            return lax.dynamic_update_index_in_dim(acc, result, block_id, 0)

        partial_sum = lax.fori_loop(first_block, last_block, add_block, partial_sum)
        split_terms = partial_sum.reshape(block_total, shard_count, local_rows, width)
        received = lax.all_to_all(split_terms, "shard", split_axis=1, concat_axis=1, tiled=True)
        mixed = jnp.sum(received, axis=1)
        updated = (carried.astype(jnp.float32) + probs[:, :, None] * mixed).astype(jnp.bfloat16)
        stored = jnp.where(segment_index == tick, updated, stored)
        if tick + 1 < segment_count:
            carried = shifted(updated, "segment", 1)
    return stored[None]


def solution(mesh):
    placed = (
        P(None, "shard", None),
        P("segment", None),
        P("segment", None, "shard"),
        P("segment", None, "shard"),
        P("segment", "shard", None),
        P("segment"),
        P("segment", None, "shard"),
    )
    return jax.shard_map(
        shards,
        mesh=mesh,
        in_specs=placed,
        out_specs=P("segment", None, "shard", None),
        check_vma=False,
    )
```

profile of v0, /device:TPU:5, one launch (start us, length us, event | category | flops | bytes accessed | tf_op | source)
XLA Modules:
  0.0 946.9 jit_solution(11908347532508689451)
XLA Ops:
  6.5 0.9 fusion.76
  7.4 0.9 fusion.78
  8.3 0.6 copy.26
  9.6 82.2 %all-gather.5.cloned.1.call-done = bf16[3,128,3072]{2,0,1:T(4,128)(2,1)} async-done(((bf16[3,2,3072]{2,0,1:T(4,128)(2,1)}), bf16[3,128,3072]{2,0,1:T(4,128)(2,1)}) %all-gather.5.cloned.1.call-update) | async-done | bytes 2359312 | tf_op jit(solution)/shard_map/all_gather | solution.py:49
  91.9 4.2 copy.27
  96.1 2.7 broadcast.59.clone
  98.9 7.1 while.40
  98.9 1.7 fusion.138
  100.6 5.4 fusion.139
  106.0 6.6 reshape.46
  112.6 6.1 copy.28
  118.6 13.8 %all-to-all-start = ((f32[3,64,2,3072]{3,2,0,1:T(2,128)}), f32[3,64,2,3072]{3,2,0,1:T(2,128)}, u32[]{:S(2)}, u32[]{:S(2)}) async-start(f32[3,64,2,3072]{3,2,0,1:T(2,128)} %copy.28), calls=%async_computation | async-start | bytes 9437184 | tf_op jit(solution)/shard_map/all_to_all | solution.py:59
  132.6 107.0 %all-to-all-done = f32[3,64,2,3072]{3,2,0,1:T(2,128)} async-done(((f32[3,64,2,3072]{3,2,0,1:T(2,128)}), f32[3,64,2,3072]{3,2,0,1:T(2,128)}, u32[]{:S(2)}, u32[]{:S(2)}) %all-to-all-start) | async-done | bytes 4718624 | tf_op jit(solution)/shard_map/all_to_all | solution.py:59
  239.6 3.7 reduce_sum.73
  243.2 0.1 fusion.79
  243.3 2.8 collective-permute-start
  246.2 1.9 collective-permute-done
  248.1 0.1 fusion.80
  248.2 0.1 fusion.82
  248.3 0.6 copy.29
  249.0 76.5 %all-gather.7.cloned.1.call-done = bf16[3,128,3072]{2,0,1:T(4,128)(2,1)} async-done(((bf16[3,2,3072]{2,0,1:T(4,128)(2,1)}), bf16[3,128,3072]{2,0,1:T(4,128)(2,1)}) %all-gather.7.cloned.1.call-update) | async-done | bytes 2359312 | tf_op jit(solution)/shard_map/all_gather | solution.py:49
  325.5 4.2 copy.30
  329.7 2.7 broadcast.59.clone.1
  332.4 7.1 while.41
  332.4 1.7 fusion.145
  334.2 5.4 fusion.146
  339.5 6.6 reshape.47
  346.1 4.0 copy.31
  350.1 120.6 %all_to_all.20 = f32[3,64,2,3072]{3,2,0,1:T(2,128)} all-to-all(f32[3,64,2,3072]{3,2,0,1:T(2,128)S(1)} %copy.31), channel_id=1, replica_groups=mesh['segment'=4,'shard'=64] {'shard'}, dimensions={1} | all-to-all | bytes 9437184 | tf_op jit(solution)/shard_map/all_to_all | solution.py:59
  470.6 3.7 reduce_sum.75
  474.3 0.1 fusion.83
  474.4 2.8 collective-permute-start.1
  477.2 1.9 collective-permute-done.1
  479.1 0.1 fusion.84
  479.3 0.1 fusion.86
  479.4 0.6 copy.32
  480.1 76.9 %all-gather.9.cloned.1.call-done = bf16[3,128,3072]{2,0,1:T(4,128)(2,1)} async-done(((bf16[3,2,3072]{2,0,1:T(4,128)(2,1)}), bf16[3,128,3072]{2,0,1:T(4,128)(2,1)}) %all-gather.9.cloned.1.call-update) | async-done | bytes 2359312 | tf_op jit(solution)/shard_map/all_gather | solution.py:49
  557.0 4.2 copy.33
  561.2 2.7 broadcast.59.clone.2
  563.9 7.1 while.42
  563.9 1.7 fusion.152
  565.6 5.4 fusion.153
  571.0 6.6 reshape.48
  577.6 4.0 copy.34
  581.6 120.6 %all_to_all.21 = f32[3,64,2,3072]{3,2,0,1:T(2,128)} all-to-all(f32[3,64,2,3072]{3,2,0,1:T(2,128)S(1)} %copy.34), channel_id=1, replica_groups=mesh['segment'=4,'shard'=64] {'shard'}, dimensions={1} | all-to-all | bytes 9437184 | tf_op jit(solution)/shard_map/all_to_all | solution.py:59
  702.1 3.7 reduce_sum.77
  705.8 0.1 fusion.87
  705.9 2.8 collective-permute-start.2
  708.7 1.9 collective-permute-done.2
  710.6 0.1 fusion.88
  710.8 0.1 fusion.90
  710.9 0.6 copy.35
  711.5 77.0 %all-gather.11.cloned.1.call-done = bf16[3,128,3072]{2,0,1:T(4,128)(2,1)} async-done(((bf16[3,2,3072]{2,0,1:T(4,128)(2,1)}), bf16[3,128,3072]{2,0,1:T(4,128)(2,1)}) %all-gather.11.cloned.1.call-update) | async-done | bytes 2359312 | tf_op jit(solution)/shard_map/all_gather | solution.py:49
  788.5 4.2 copy.36
  792.7 2.7 broadcast.59
  795.4 7.1 while.43
  795.4 1.7 fusion.159
  797.2 5.4 fusion.160
  802.5 6.6 reshape.49
  809.1 6.1 copy.37
  815.2 13.7 %all-to-all-start.3 = ((f32[3,64,2,3072]{3,2,0,1:T(2,128)}), f32[3,64,2,3072]{3,2,0,1:T(2,128)}, u32[]{:S(2)}, u32[]{:S(2)}) async-start(f32[3,64,2,3072]{3,2,0,1:T(2,128)} %copy.37), calls=%async_computation.3 | async-start | bytes 9437184 | tf_op jit(solution)/shard_map/all_to_all | solution.py:59
  828.9 107.1 %all-to-all-done.3 = f32[3,64,2,3072]{3,2,0,1:T(2,128)} async-done(((f32[3,64,2,3072]{3,2,0,1:T(2,128)}), f32[3,64,2,3072]{3,2,0,1:T(2,128)}, u32[]{:S(2)}, u32[]{:S(2)}) %all-to-all-start.3) | async-done | bytes 4718624 | tf_op jit(solution)/shard_map/all_to_all | solution.py:59
  936.0 3.7 reduce_sum.79
  939.7 0.7 fusion.92
  (25 shorter events, 0.4 us)
Async XLA Ops:
  6.5 85.3 %all-gather.5.cloned.1.call-start = ((), (), s32[]{:S(2)}) async-start(), calls=%async_computation.4 | async-start | bytes 3194880 | tf_op jit(solution)/shard_map/all_gather | solution.py:49
  96.1 2.8 copy-start
  118.6 13.9 %copy-start.5 = (f32[1,3,2]{1,2,0:T(2,128)S(1)}, f32[1,3,2]{1,2,0:T(2,128)}, u32[]{:S(2)}) copy-start(f32[1,3,2]{1,2,0:T(2,128)} %param.21) | copy-start | bytes 76
  118.6 120.9 %all-to-all-start = ((f32[3,64,2,3072]{3,2,0,1:T(2,128)}), f32[3,64,2,3072]{3,2,0,1:T(2,128)}, u32[]{:S(2)}, u32[]{:S(2)}) async-start(f32[3,64,2,3072]{3,2,0,1:T(2,128)} %copy.28), calls=%async_computation | async-start | bytes 9437184 | tf_op jit(solution)/shard_map/all_to_all | solution.py:59
  132.4 110.8 %copy-start.1 = (bf16[3,2,3072]{2,1,0:T(2,128)(2,1)S(1)}, bf16[3,2,3072]{2,1,0:T(2,128)(2,1)}, u32[]{:S(2)}) copy-start(bf16[3,2,3072]{2,1,0:T(2,128)(2,1)} %param.15) | copy-start | bytes 110596
  132.4 115.8 %copy-start.2 = (f32[1,3072]{1,0:T(1,128)S(1)}, f32[1,3072]{1,0:T(1,128)}, u32[]{:S(2)}) copy-start(f32[1,3072]{1,0:T(1,128)} %param.16) | copy-start | bytes 36868
  132.4 193.1 %all-gather.7.cloned.1.call-start = ((), (), s32[]{:S(2)}) async-start(), calls=%async_computation.5 | async-start | bytes 3194880 | tf_op jit(solution)/shard_map/all_gather | solution.py:49
  243.3 4.7 collective-permute-start
  249.0 308.0 %all-gather.9.cloned.1.call-start = ((), (), s32[]{:S(2)}) async-start(), calls=%async_computation.6 | async-start | bytes 3194880 | tf_op jit(solution)/shard_map/all_gather | solution.py:49
  474.4 4.7 collective-permute-start.1
  480.0 308.5 %all-gather.11.cloned.1.call-start = ((), (), s32[]{:S(2)}) async-start(), calls=%async_computation.7 | async-start | bytes 3194880 | tf_op jit(solution)/shard_map/all_gather | solution.py:49
  705.9 89.5 %copy-start.3 = (bf16[3,2,3072]{2,1,0:T(2,128)(2,1)}, bf16[3,2,3072]{2,1,0:T(2,128)(2,1)S(1)}, u32[]{:S(2)}) copy-start(bf16[3,2,3072]{2,1,0:T(2,128)(2,1)S(1)} %fusion.87) | copy-start | bytes 110596
  705.9 4.7 collective-permute-start.2
  815.2 120.8 %all-to-all-start.3 = ((f32[3,64,2,3072]{3,2,0,1:T(2,128)}), f32[3,64,2,3072]{3,2,0,1:T(2,128)}, u32[]{:S(2)}, u32[]{:S(2)}) async-start(f32[3,64,2,3072]{3,2,0,1:T(2,128)} %copy.37), calls=%async_computation.3 | async-start | bytes 9437184 | tf_op jit(solution)/shard_map/all_to_all | solution.py:59
  828.8 110.8 %copy-start.4 = (bf16[3,2,3072]{2,1,0:T(2,128)(2,1)S(1)}, bf16[3,2,3072]{2,1,0:T(2,128)(2,1)}, u32[]{:S(2)}) copy-start(bf16[3,2,3072]{2,1,0:T(2,128)(2,1)} %copy-done.3) | copy-start | bytes 110596
Sparse Core Ops, SparseCore 0:
  10.1 81.7 all-gather.4
  249.1 76.3 all-gather.6
  480.1 76.8 all-gather.8
  711.6 76.8 all-gather.10
where the time goes:
time: 949 us; the launch traced here: 947 us
  waiting for transfers between devices  532 us (56%)
  blocking collectives  241 us (25%)
  local copies, waits for them, and re-layouts  76.8 us (8%)
  starting transfers between devices  36 us (4%)
  matrix products  28.3 us (3%)
  other arithmetic  18.2 us (2%)
  between operations  14 us (1%)
    all_gather x4, waiting for transfers between devices, shards(): gathered = lax.all_gather(normed, 'shard', axis=1, tiled=True)  313 us
    all_to_all x2, blocking collectives, shards(): lax.all_to_all(split_terms, 'shard', split_axis=1, concat_axis=1, tiled=T...  241 us
    all_to_all x2, waiting for transfers between devices, shards(): lax.all_to_all(split_terms, 'shard', split_axis=1, concat_axis=1, tiled=T...  214 us
    reshape x8, local copies, waits for them, and re-layouts, shards(): partial_sum.reshape(block_total, shard_count, local_rows, width)  46.4 us
    all_to_all x2, starting transfers between devices, shards(): lax.all_to_all(split_terms, 'shard', split_axis=1, concat_axis=1, tiled=T...  27.4 us
    dot_general x4, matrix products, expert_rows(): return jnp.dot(hidden, down_part, preferred_element_type=jnp.float32)  21.5 us
  transfers between devices with their start and end apart: 9, of which 9 were waited for; matrix products, arithmetic and copies ran while one was open for 0% of the time, Pallas kernels for 0%

commit v1 on v0

--- a/solution.py
+++ b/solution.py
@@ -46,7 +46,8 @@
     stored = jnp.zeros_like(tokens)
     for tick in range(segment_count):
         normed = normalize(carried, row_gain)
-        gathered = lax.all_gather(normed, "shard", axis=1, tiled=True)
+        copies = jnp.concatenate([normed] * lax.axis_size("shard"), axis=1)
+        gathered = lax.all_to_all(copies, "shard", 1, 1, tiled=True)
         partial_sum = jnp.zeros(gathered.shape, jnp.float32)
 
         def add_block(block_id, acc):

time: 949 us -> 1040 us (1.096)
  waiting for transfers between devices: 532 us -> 439 us
  local copies, waits for them, and re-layouts: 76.8 us -> 160 us
  blocking collectives: 241 us -> 321 us
  starting transfers between devices: 36 us -> 62.8 us
  between operations: 14 us -> 1.1 us
    all_gather x4 -> x0, waiting for transfers between devices: 313 us -> none  [shards(): gathered = lax.all_gather(normed, 'shard', axis=1, tiled=True)]
    all_to_all x0 -> x3, waiting for transfers between devices: none -> 220 us  [shards(): gathered = lax.all_to_all(copies, 'shard', 1, 1, tiled=True)]
    concatenate x0 -> x8, local copies, waits for them, and re-layouts: none -> 89.5 us  [shards(): copies = jnp.concatenate([normed] * lax.axis_size('shard'), axis=1)]
    all_to_all x0 -> x1, blocking collectives: none -> 80.7 us  [shards(): gathered = lax.all_to_all(copies, 'shard', 1, 1, tiled=True)]
    all_to_all x0 -> x3, starting transfers between devices: none -> 27.1 us  [shards(): gathered = lax.all_to_all(copies, 'shard', 1, 1, tiled=True)]
  transfers between devices with their start and end apart: 9 -> 8, of which waited for: 9 -> 8; matrix products, arithmetic and copies ran while one was open for 0% -> 0% of each run, Pallas kernels for 0% -> 0%
where the time goes in v1:
time: 1040 us; the launch traced here: 1030 us
  waiting for transfers between devices  439 us (42%)
  blocking collectives  321 us (31%)
  local copies, waits for them, and re-layouts  160 us (15%)
  starting transfers between devices  62.8 us (6%)
  matrix products  28.3 us (3%)
  other arithmetic  18.2 us (2%)
    all_to_all x2, blocking collectives, shards(): lax.all_to_all(split_terms, 'shard', split_axis=1, concat_axis=1, tiled=T...  241 us
    all_to_all x3, waiting for transfers between devices, shards(): gathered = lax.all_to_all(copies, 'shard', 1, 1, tiled=True)  220 us
    all_to_all x2, waiting for transfers between devices, shards(): lax.all_to_all(split_terms, 'shard', split_axis=1, concat_axis=1, tiled=T...  214 us
    concatenate x8, local copies, waits for them, and re-layouts, shards(): copies = jnp.concatenate([normed] * lax.axis_size('shard'), axis=1)  89.5 us
    all_to_all x1, blocking collectives, shards(): gathered = lax.all_to_all(copies, 'shard', 1, 1, tiled=True)  80.7 us
    reshape x8, local copies, waits for them, and re-layouts, shards(): partial_sum.reshape(block_total, shard_count, local_rows, width)  46.5 us
    all_to_all x2, starting transfers between devices, shards(): lax.all_to_all(split_terms, 'shard', split_axis=1, concat_axis=1, tiled=T...  27.2 us
    all_to_all x3, starting transfers between devices, shards(): gathered = lax.all_to_all(copies, 'shard', 1, 1, tiled=True)  27.1 us
  transfers between devices with their start and end apart: 8, of which 8 were waited for; matrix products, arithmetic and copies ran while one was open for 0% of the time, Pallas kernels for 0%

profile of v1, /device:TPU:5, one launch (start us, length us, event | category | flops | bytes accessed | tf_op | source)
XLA Modules:
  0.0 1031.8 jit_solution(8767574746925726564)
XLA Ops:
  0.0 0.9 fusion.76
  0.9 0.9 fusion.78
  1.8 4.9 concatenate.12
  6.7 3.7 copy.26
  10.4 12.3 %all-to-all-start = ((bf16[3,128,3072]{2,0,1:T(4,128)(2,1)}), bf16[3,128,3072]{2,0,1:T(4,128)(2,1)S(1)}, u32[]{:S(2)}, u32[]{:S(2)}) async-start(bf16[3,128,3072]{2,0,1:T(4,128)(2,1)} %copy.26), calls=%async_computation | async-start | bytes 6291456 | tf_op jit(solution)/shard_map/all_to_all | solution.py:50
  23.4 72.8 %all-to-all-done = bf16[3,128,3072]{2,0,1:T(4,128)(2,1)S(1)} async-done(((bf16[3,128,3072]{2,0,1:T(4,128)(2,1)}), bf16[3,128,3072]{2,0,1:T(4,128)(2,1)S(1)}, u32[]{:S(2)}, u32[]{:S(2)}) %all-to-all-start) | async-done | bytes 2359328 | tf_op jit(solution)/shard_map/all_to_all | solution.py:50
  96.3 2.3 copy.27
  98.6 2.7 broadcast.59.clone
  101.4 7.1 while.40
  101.4 1.7 fusion.138
  103.1 5.4 fusion.139
  108.5 6.6 reshape.46
  115.1 6.1 copy.28
  121.2 13.8 %all-to-all-start.1 = ((f32[3,64,2,3072]{3,2,0,1:T(2,128)}), f32[3,64,2,3072]{3,2,0,1:T(2,128)}, u32[]{:S(2)}, u32[]{:S(2)}) async-start(f32[3,64,2,3072]{3,2,0,1:T(2,128)} %copy.28), calls=%async_computation.1 | async-start | bytes 9437184 | tf_op jit(solution)/shard_map/all_to_all | solution.py:60
  135.1 106.8 %all-to-all-done.1 = f32[3,64,2,3072]{3,2,0,1:T(2,128)} async-done(((f32[3,64,2,3072]{3,2,0,1:T(2,128)}), f32[3,64,2,3072]{3,2,0,1:T(2,128)}, u32[]{:S(2)}, u32[]{:S(2)}) %all-to-all-start.1) | async-done | bytes 4718624 | tf_op jit(solution)/shard_map/all_to_all | solution.py:60
  241.9 3.7 reduce_sum.73
  245.7 2.8 collective-permute-start
  248.5 1.9 collective-permute-done
  250.4 0.1 fusion.80
  250.6 22.1 %concatenate.13 = bf16[3,128,3072]{2,1,0:T(8,128)(2,1)} concatenate(bf16[3,2,3072]{2,1,0:T(2,128)(2,1)S(1)} %fusion.82, bf16[3,2,3072]{2,1,0:T(2,128)(2,1)S(1)} %fusion.82, bf16[3,2,3072]{2,1,0:T(2,128)(2,1)S(1)} %fusion.82, bf16[3,2,3072]{2,1,0:T(2,128)(2,1)S(1)} %fusion.82, bf16[3,2,3072]{2,1,0:T(2,128)(2,1)S(1)} %fusion.82, bf16[3,2,3072]{2,1,0:T(2,128)(2,1)S(1)} %fusion.82, ...), dimensions={1} | concatenate | bytes 4718592 | tf_op jit(solution)/shard_map/concatenate | solution.py:49
  272.8 5.4 copy.29
  278.2 7.2 all-to-all-start.2
  285.3 73.4 %all-to-all-done.2 = bf16[3,128,3072]{2,0,1:T(4,128)(2,1)} async-done(((bf16[3,128,3072]{2,0,1:T(4,128)(2,1)}), bf16[3,128,3072]{2,0,1:T(4,128)(2,1)}, u32[]{:S(2)}, u32[]{:S(2)}) %all-to-all-start.2) | async-done | bytes 2359328 | tf_op jit(solution)/shard_map/all_to_all | solution.py:50
  358.8 4.2 copy.30
  363.0 2.7 broadcast.59.clone.1
  365.7 7.1 while.41
  365.7 1.7 fusion.145
  367.4 5.4 fusion.146
  372.8 6.6 reshape.47
  379.4 4.0 copy.31
  383.3 120.5 %all_to_all.41 = f32[3,64,2,3072]{3,2,0,1:T(2,128)} all-to-all(f32[3,64,2,3072]{3,2,0,1:T(2,128)S(1)} %copy.31), channel_id=1, replica_groups=mesh['segment'=4,'shard'=64] {'shard'}, dimensions={1} | all-to-all | bytes 9437184 | tf_op jit(solution)/shard_map/all_to_all | solution.py:60
  503.8 3.7 reduce_sum.75
  507.6 2.8 collective-permute-start.1
  510.4 1.8 collective-permute-done.1
  512.3 0.1 fusion.84
  512.5 22.1 %concatenate.14 = bf16[3,128,3072]{2,1,0:T(8,128)(2,1)} concatenate(bf16[3,2,3072]{2,1,0:T(2,128)(2,1)S(1)} %fusion.86, bf16[3,2,3072]{2,1,0:T(2,128)(2,1)S(1)} %fusion.86, bf16[3,2,3072]{2,1,0:T(2,128)(2,1)S(1)} %fusion.86, bf16[3,2,3072]{2,1,0:T(2,128)(2,1)S(1)} %fusion.86, bf16[3,2,3072]{2,1,0:T(2,128)(2,1)S(1)} %fusion.86, bf16[3,2,3072]{2,1,0:T(2,128)(2,1)S(1)} %fusion.86, ...), dimensions={1} | concatenate | bytes 4718592 | tf_op jit(solution)/shard_map/concatenate | solution.py:49
  534.7 5.4 copy.32
  540.1 7.6 all-to-all-start.4
  547.7 73.4 %all-to-all-done.4 = bf16[3,128,3072]{2,0,1:T(4,128)(2,1)} async-done(((bf16[3,128,3072]{2,0,1:T(4,128)(2,1)}), bf16[3,128,3072]{2,0,1:T(4,128)(2,1)}, u32[]{:S(2)}, u32[]{:S(2)}) %all-to-all-start.4) | async-done | bytes 2359328 | tf_op jit(solution)/shard_map/all_to_all | solution.py:50
  621.1 4.2 copy.33
  625.3 2.7 broadcast.59.clone.2
  628.0 7.5 while.42
  628.0 1.7 fusion.152
  629.7 5.4 fusion.153
  635.5 6.6 reshape.48
  642.1 4.0 copy.34
  646.1 120.3 %all_to_all.42 = f32[3,64,2,3072]{3,2,0,1:T(2,128)} all-to-all(f32[3,64,2,3072]{3,2,0,1:T(2,128)S(1)} %copy.34), channel_id=1, replica_groups=mesh['segment'=4,'shard'=64] {'shard'}, dimensions={1} | all-to-all | bytes 9437184 | tf_op jit(solution)/shard_map/all_to_all | solution.py:60
  766.3 3.7 reduce_sum.77
  770.1 2.8 collective-permute-start.2
  773.0 1.8 collective-permute-done.2
  775.1 22.1 %concatenate.15 = bf16[3,128,3072]{2,1,0:T(8,128)(2,1)} concatenate(bf16[3,2,3072]{2,1,0:T(2,128)(2,1)S(1)} %fusion.90, bf16[3,2,3072]{2,1,0:T(2,128)(2,1)S(1)} %fusion.90, bf16[3,2,3072]{2,1,0:T(2,128)(2,1)S(1)} %fusion.90, bf16[3,2,3072]{2,1,0:T(2,128)(2,1)S(1)} %fusion.90, bf16[3,2,3072]{2,1,0:T(2,128)(2,1)S(1)} %fusion.90, bf16[3,2,3072]{2,1,0:T(2,128)(2,1)S(1)} %fusion.90, ...), dimensions={1} | concatenate | bytes 4718592 | tf_op jit(solution)/shard_map/concatenate | solution.py:49
  797.2 3.7 copy.35
  800.9 80.7 %all_to_all.40 = bf16[3,128,3072]{2,0,1:T(4,128)(2,1)S(1)} all-to-all(bf16[3,128,3072]{2,0,1:T(4,128)(2,1)S(1)} %copy.35), channel_id=1, replica_groups=mesh['segment'=4,'shard'=64] {'shard'}, dimensions={1} | all-to-all | bytes 4718592 | tf_op jit(solution)/shard_map/all_to_all | solution.py:50
  881.6 2.3 copy.36
  884.0 2.7 broadcast.59
  886.7 7.3 while.43
  886.8 1.7 fusion.159
  888.5 5.4 fusion.160
  893.9 6.6 reshape.49
  900.5 6.1 copy.37
  906.6 13.4 %all-to-all-start.7 = ((f32[3,64,2,3072]{3,2,0,1:T(2,128)}), f32[3,64,2,3072]{3,2,0,1:T(2,128)}, u32[]{:S(2)}, u32[]{:S(2)}) async-start(f32[3,64,2,3072]{3,2,0,1:T(2,128)} %copy.37), calls=%async_computation.7 | async-start | bytes 9437184 | tf_op jit(solution)/shard_map/all_to_all | solution.py:60
  920.0 107.1 %all-to-all-done.7 = f32[3,64,2,3072]{3,2,0,1:T(2,128)} async-done(((f32[3,64,2,3072]{3,2,0,1:T(2,128)}), f32[3,64,2,3072]{3,2,0,1:T(2,128)}, u32[]{:S(2)}, u32[]{:S(2)}) %all-to-all-start.7) | async-done | bytes 4718624 | tf_op jit(solution)/shard_map/all_to_all | solution.py:60
  1027.2 3.7 reduce_sum.79
  1030.8 0.7 fusion.92
  (24 shorter events, 1.0 us)
Async XLA Ops:
  10.4 85.8 %all-to-all-start = ((bf16[3,128,3072]{2,0,1:T(4,128)(2,1)}), bf16[3,128,3072]{2,0,1:T(4,128)(2,1)S(1)}, u32[]{:S(2)}, u32[]{:S(2)}) async-start(bf16[3,128,3072]{2,0,1:T(4,128)(2,1)} %copy.26), calls=%async_computation | async-start | bytes 6291456 | tf_op jit(solution)/shard_map/all_to_all | solution.py:50
  98.6 2.8 copy-start
  121.2 13.8 %copy-start.5 = (f32[1,3,2]{1,2,0:T(2,128)S(1)}, f32[1,3,2]{1,2,0:T(2,128)}, u32[]{:S(2)}) copy-start(f32[1,3,2]{1,2,0:T(2,128)} %param.21) | copy-start | bytes 76
  121.2 120.7 %all-to-all-start.1 = ((f32[3,64,2,3072]{3,2,0,1:T(2,128)}), f32[3,64,2,3072]{3,2,0,1:T(2,128)}, u32[]{:S(2)}, u32[]{:S(2)}) async-start(f32[3,64,2,3072]{3,2,0,1:T(2,128)} %copy.28), calls=%async_computation.1 | async-start | bytes 9437184 | tf_op jit(solution)/shard_map/all_to_all | solution.py:60
  134.9 110.6 %copy-start.1 = (bf16[3,2,3072]{2,1,0:T(2,128)(2,1)S(1)}, bf16[3,2,3072]{2,1,0:T(2,128)(2,1)}, u32[]{:S(2)}) copy-start(bf16[3,2,3072]{2,1,0:T(2,128)(2,1)} %param.15) | copy-start | bytes 110596
  135.0 115.6 %copy-start.2 = (f32[1,3072]{1,0:T(1,128)S(1)}, f32[1,3072]{1,0:T(1,128)}, u32[]{:S(2)}) copy-start(f32[1,3072]{1,0:T(1,128)} %param.16) | copy-start | bytes 36868
  245.7 4.7 collective-permute-start
  278.2 80.6 %all-to-all-start.2 = ((bf16[3,128,3072]{2,0,1:T(4,128)(2,1)}), bf16[3,128,3072]{2,0,1:T(4,128)(2,1)}, u32[]{:S(2)}, u32[]{:S(2)}) async-start(bf16[3,128,3072]{2,0,1:T(4,128)(2,1)} %copy.29), calls=%async_computation.2 | async-start | bytes 6291456 | tf_op jit(solution)/shard_map/all_to_all | solution.py:50
  507.6 4.7 collective-permute-start.1
  540.1 81.0 %all-to-all-start.4 = ((bf16[3,128,3072]{2,0,1:T(4,128)(2,1)}), bf16[3,128,3072]{2,0,1:T(4,128)(2,1)}, u32[]{:S(2)}, u32[]{:S(2)}) async-start(bf16[3,128,3072]{2,0,1:T(4,128)(2,1)} %copy.32), calls=%async_computation.4 | async-start | bytes 6291456 | tf_op jit(solution)/shard_map/all_to_all | solution.py:50
  770.1 30.8 %copy-start.3 = (bf16[3,2,3072]{2,1,0:T(2,128)(2,1)}, bf16[3,2,3072]{2,1,0:T(2,128)(2,1)S(1)}, u32[]{:S(2)}) copy-start(bf16[3,2,3072]{2,1,0:T(2,128)(2,1)S(1)} %fusion.87) | copy-start | bytes 110596
  770.1 4.7 collective-permute-start.2
  906.6 120.6 %all-to-all-start.7 = ((f32[3,64,2,3072]{3,2,0,1:T(2,128)}), f32[3,64,2,3072]{3,2,0,1:T(2,128)}, u32[]{:S(2)}, u32[]{:S(2)}) async-start(f32[3,64,2,3072]{3,2,0,1:T(2,128)} %copy.37), calls=%async_computation.7 | async-start | bytes 9437184 | tf_op jit(solution)/shard_map/all_to_all | solution.py:60
  920.0 110.8 %copy-start.4 = (bf16[3,2,3072]{2,1,0:T(2,128)(2,1)S(1)}, bf16[3,2,3072]{2,1,0:T(2,128)(2,1)}, u32[]{:S(2)}) copy-start(bf16[3,2,3072]{2,1,0:T(2,128)(2,1)} %copy-done.3) | copy-start | bytes 110596
